TPU v7x, 256 devices: a whole 4x4x8 slice. The times are simulated.
256 devices in a mesh: grp: 128 (over z, x, y), rep: 2 (over core).
Axes of the slice: x: 4, y: 4, z: 8, core: 2. Of those that a mesh axis runs over, the one named last changes fastest.
Arguments:
- snapshots: float32 [128, 2048, 1024], P('grp', 'rep'), may hold values from -6 to 6
- row_factor: float32 [2048, 128], P('rep'), may hold values from -0.125 to 0.125
- time_factor: float32 [128, 64], replicated, may hold values from -0.5 to 0.5
Outputs:
- new_rows: float32 [2048, 128], P('rep')
- new_time: float32 [128, 64], replicated
All inputs are finite; a program needn't handle non-finite values.
Results may differ from a plain program's by a relative error of at most 0.0001.
Values sent between devices are 32-bit elements; how exact they have to be, the bound alone decides.
A program may use at most 64 MiB of HBM per device.

v0:
```python
import math

import jax
import jax.numpy as jnp
from jax import lax
from jax.sharding import PartitionSpec as P

ROWS = 2048
STEPS = 8


def highdot(left, right):
    return jnp.dot(left, right, precision=lax.Precision.HIGHEST, preferred_element_type=jnp.float32)


def orthogonalize(start_matrix):
    total = jnp.sum(start_matrix * start_matrix)
    iterate = start_matrix / jnp.sqrt(total + 1e-06)
    for step_index in range(STEPS):
        inner = highdot(iterate.T, iterate)
        iterate = 1.5 * iterate - 0.5 * highdot(iterate, inner)
    return iterate


def on_device(snapshots, row_factor, time_factor):
    row_half = snapshots.shape[1]
    rank_row = row_factor.shape[1]
    projected = jnp.einsum("tij,ia->tja", snapshots, row_factor, precision=lax.Precision.HIGHEST)
    summed = lax.psum(projected, "rep")
    owned = lax.all_to_all(summed, "grp", split_axis=1, concat_axis=0, tiled=True)
    snaps = owned.shape[0]
    width = owned.shape[1] * rank_row
    flat = owned.reshape(snaps, width)
    halfwidth = width // 2
    portion = lax.dynamic_slice_in_dim(flat, lax.axis_index("rep") * halfwidth, halfwidth, 1)
    gram_part = highdot(portion, portion.T)
    gram_total = lax.psum(gram_part, ("grp", "rep"))
    start_time = highdot(gram_total, time_factor)
    basis_time = orthogonalize(start_time)
    mixer = highdot(basis_time, basis_time.T)
    weights = highdot(mixer, flat).reshape(owned.shape)
    returned = lax.all_to_all(weights, "grp", split_axis=0, concat_axis=1, tiled=True)
    own_rows = lax.psum_scatter(
        jnp.einsum("tij,tja->ia", snapshots, returned, precision=lax.Precision.HIGHEST),
        "grp",
        scatter_dimension=0,
        tiled=True,
    )
    half_block = lax.all_gather(own_rows, "grp", axis=0, tiled=True)
    all_block = lax.all_gather(half_block, "rep", axis=0, tiled=True)
    basis = orthogonalize(all_block)
    new_rows = lax.dynamic_slice_in_dim(basis, lax.axis_index("rep") * row_half, row_half, 0)
    return (new_rows * math.sqrt(ROWS), basis_time * math.sqrt(snaps))


def solution(mesh):
    return jax.shard_map(
        on_device,
        mesh=mesh,
        in_specs=(P("grp", "rep", None), P("rep", None), P()),
        out_specs=(P("rep", None), P()),
        check_vma=False,
    )
```

profile of v0, /device:TPU:1, one launch (start us, length us, event | category | flops | bytes accessed | tf_op | source)
XLA Modules:
  0.0 982.7 jit_solution(4008514134810224522)
XLA Ops:
  7.2 1.0 copy-done
  8.2 9.6 fusion.11
  17.9 34.2 %all-reduce.5.cloned.1.call-done = f32[1,1024,128]{2,1,0:T(8,128)} async-done(((f32[1,1024,128]{2,1,0:T(8,128)}), f32[1,1024,128]{2,1,0:T(8,128)}) %all-reduce.5.cloned.1.call-update) | async-done | bytes 524304 | tf_op jit(solution)/shard_map/psum | solution.py:29
  52.1 13.6 %all-to-all-start = ((f32[1,1024,128]{2,0,1:T(1,128)}), f32[1,1024,128]{2,0,1:T(1,128)S(1)}, u32[]{:S(2)}, u32[]{:S(2)}) async-start(f32[1,1024,128]{2,0,1:T(1,128)} %bitcast.92), calls=%async_computation | async-start | bytes 1048576 | tf_op jit(solution)/shard_map/all_to_all | solution.py:30
  65.7 19.0 %all-to-all-done = f32[1,1024,128]{2,0,1:T(1,128)S(1)} async-done(((f32[1,1024,128]{2,0,1:T(1,128)}), f32[1,1024,128]{2,0,1:T(1,128)S(1)}, u32[]{:S(2)}, u32[]{:S(2)}) %all-to-all-start) | async-done | bytes 524320 | tf_op jit(solution)/shard_map/all_to_all | solution.py:30
  84.6 0.5 broadcast.53
  85.2 1.9 reduce.3
  87.1 1.0 fusion.29
  88.2 0.2 all-reduce.9.cloned.1.call-start
  88.4 0.2 copy.27
  88.6 232.1 %all-reduce.7.cloned.1.call-done = f32[128,128]{1,0:T(8,128)} async-done(((f32[128,128]{1,0:T(8,128)}), f32[128,128]{1,0:T(8,128)}) %all-reduce.7.cloned.1.call-update) | async-done | bytes 65552 | tf_op jit(solution)/shard_map/psum | solution.py:37
  320.7 1.7 multiply_reduce_fusion.1
  323.3 0.2 fusion.24
  323.7 0.2 fusion.23
  324.2 0.2 fusion.22
  324.6 0.2 fusion.21
  325.0 0.2 fusion.20
  325.5 0.2 fusion.19
  325.9 0.2 fusion.18
  326.3 0.9 broadcast_multiply_fusion
  327.2 0.3 convolution_bitcast_fusion
  327.5 0.6 fusion.40
  328.1 0.3 copy.28
  328.4 25.9 %all_to_all.8 = f32[128,8,128]{2,1,0:T(8,128)S(1)} all-to-all(f32[128,8,128]{2,1,0:T(8,128)S(1)} %copy.28), channel_id=1, replica_groups=mesh['grp'=128,'rep'=2] {'grp'}, dimensions={0} | all-to-all | bytes 1048576 | tf_op jit(solution)/shard_map/all_to_all | solution.py:42
  354.3 5.4 fusion.14
  359.8 0.6 dynamic-slice
  360.9 206.4 %all-reduce.9.cloned.1.call-done = f32[1024,128]{0,1:T(8,128)} async-done(((f32[1024,128]{0,1:T(8,128)}), f32[1024,128]{0,1:T(8,128)}) %all-reduce.9.cloned.1.call-update) | async-done | bytes 524304
  567.3 0.9 constant_dynamic-slice_fusion
  568.3 309.9 %all_gather.6 = f32[1024,128]{1,0:T(8,128)} all-gather(f32[8,128]{1,0:T(8,128)S(1)} %copy.29), channel_id=1, replica_groups=mesh['grp'=128,'rep'=2] {'grp'}, dimensions={0}, use_global_device_ids=true | all-gather | bytes 528384 | tf_op jit(solution)/shard_map/all_gather | solution.py:49
  878.2 69.5 %all-gather.2.cloned.1.call-done = f32[2048,128]{1,0:T(8,128)} async-done(((f32[1024,128]{1,0:T(8,128)}), f32[2048,128]{1,0:T(8,128)}) %all-gather.2.cloned.1.call-update) | async-done | bytes 1048592 | tf_op jit(solution)/shard_map/all_gather | solution.py:50
  947.7 2.2 multiply_reduce_fusion
  950.6 3.4 fusion.28
  954.0 1.0 fusion.10
  955.0 1.8 fusion.41
  956.8 1.0 fusion.9
  957.8 1.8 fusion.42
  959.6 1.0 fusion.8
  960.6 1.8 fusion.43
  962.4 1.2 fusion.7
  963.6 1.8 fusion.44
  965.5 1.0 fusion.6
  966.5 1.8 fusion.45
  968.3 1.0 fusion.5
  969.3 1.8 fusion.46
  971.1 1.0 fusion.4
  972.1 1.8 fusion.47
  973.9 1.0 fusion.48
  974.9 0.9 fusion.26
  (26 shorter events, 1.8 us)
Async XLA Ops:
  7.2 1.0 copy-start
  7.2 313.5 %copy-start.3 = (f32[128,64]{0,1:T(8,128)S(1)}, f32[128,64]{0,1:T(8,128)}, u32[]{:S(2)}) copy-start(f32[128,64]{0,1:T(8,128)} %param.5) | copy-start | bytes 98308
  7.2 44.9 %all-reduce.5.cloned.1.call-start = ((), (), s32[]{:S(2)}) async-start(), calls=%async_computation.2 | async-start | bytes 1048576 | tf_op jit(solution)/shard_map/psum | solution.py:29
  52.1 32.6 %all-to-all-start = ((f32[1,1024,128]{2,0,1:T(1,128)}), f32[1,1024,128]{2,0,1:T(1,128)S(1)}, u32[]{:S(2)}, u32[]{:S(2)}) async-start(f32[1,1024,128]{2,0,1:T(1,128)} %bitcast.92), calls=%async_computation | async-start | bytes 1048576 | tf_op jit(solution)/shard_map/all_to_all | solution.py:30
  65.6 255.1 %all-reduce.7.cloned.1.call-start = ((), (), s32[]{:S(2)}) async-start(), calls=%async_computation.3 | async-start | bytes 131072 | tf_op jit(solution)/shard_map/psum | solution.py:37
  88.2 479.1 %all-reduce.9.cloned.1.call-start = ((), (), s32[]{:S(2)}) async-start(), calls=%async_computation.5 | async-start | bytes 1048576
  323.1 31.2 %copy-start.1 = (f32[1,1024,1024]{2,1,0:T(8,128)S(1)}, f32[1,1024,1024]{2,1,0:T(8,128)}, u32[]{:S(2)}) copy-start(f32[1,1024,1024]{2,1,0:T(8,128)} %param.3) | copy-start | bytes 12582916
  328.1 31.7 %copy-start.4 = (u32[256]{0:T(256)S(1)}, u32[256]{0:T(256)}, u32[]{:S(2)}) copy-start(u32[256]{0:T(256)} %constant.29) | copy-start | bytes 3076
  359.7 588.0 %all-gather.2.cloned.1.call-start = ((), (), s32[]{:S(2)}) async-start(), calls=%async_computation.4 | async-start | bytes 1572864 | tf_op jit(solution)/shard_map/all_gather | solution.py:50
  947.7 6.3 copy-start.2
Sparse Core Ops, SparseCore 0:
  18.0 34.0 all-reduce.4
  88.3 232.3 all-reduce.6
  359.8 207.4 all-reduce.8
  878.3 69.3 all-gather.1
where the time goes:
time: 990 us; the launch traced here: 983 us
  waiting for transfers between devices  561 us (57%)
  blocking collectives  336 us (34%)
  matrix products  46.8 us (5%)
  between operations  16.5 us (2%)
  starting transfers between devices  13.9 us (1%)
    all_gather x1, blocking collectives, on_device(): half_block = lax.all_gather(own_rows, 'grp', axis=0, tiled=True)  310 us
    psum x1, waiting for transfers between devices, on_device(): gram_total = lax.psum(gram_part, ('grp', 'rep'))  232 us
    unnamed x5, waiting for transfers between devices  206 us
    all_gather x1, waiting for transfers between devices, on_device(): all_block = lax.all_gather(half_block, 'rep', axis=0, tiled=True)  69.5 us
    psum x1, waiting for transfers between devices, on_device(): summed = lax.psum(projected, 'rep')  34.2 us
    dot_general x36, matrix products, highdot(): jnp.dot(left, right, precision=lax.Precision.HIGHEST, preferred_element_t...  31.7 us
    all_to_all x1, blocking collectives, on_device(): lax.all_to_all(weights, 'grp', split_axis=0, concat_axis=1, tiled=True)  25.9 us
  transfers between devices with their start and end apart: 5, of which 5 were waited for; matrix products, arithmetic and copies ran while one was open for 0% of the time, Pallas kernels for 0%

commit v1 on v0

v1 whole, which is shorter than its diff:
```python
import functools
import math

import jax
import jax.numpy as jnp
from jax import lax
from jax.experimental import pallas as pl
from jax.experimental.pallas import tpu as pltpu
from jax.sharding import PartitionSpec as P

MESH = pl.DeviceIdType.MESH
STEPS = 8
ZS = 8
F32 = jnp.float32
BF16 = jnp.bfloat16
NN = (((1,), (0,)), ((), ()))
NT = (((1,), (1,)), ((), ()))


def full(left, right, dims=NN):
    return lax.dot_general(left, right, dims, precision=lax.Precision.HIGHEST, preferred_element_type=F32)


def half(left, right, dims=NN):
    return lax.dot_general(left, right, dims, preferred_element_type=F32)


def split(value):
    high = value.astype(BF16)
    return high, (value - high.astype(F32)).astype(BF16)


def pair(first, second):
    upper = lax.broadcasted_iota(jnp.int32, first.shape, 0) < 4
    return (
        jnp.where(upper, first, pltpu.roll(second, 4, 0)),
        jnp.where(upper, pltpu.roll(first, 4, 0), second),
    )


def kernel(nz, snap_ref, row_ref, time_ref, rows_out, time_out,
           snap, shigh, slow, proj, other, piece, plane_in, zsend, owned,
           tpart, tother, tchip, tz, tsum, tplane, tall,
           wback, wz, wsend, wpieces, whigh, wlow,
           prod, pin, psum, pz, xall, gpart, gother,
           load_sem, core_s, core_r, plane_s, plane_r, z_s, z_r):
    count = lax.axis_size("grp")
    nplane = count // nz
    me = lax.axis_index("grp")
    rep = lax.axis_index("rep")
    zi, pi = me // nplane, me % nplane
    sibling = 1 - rep
    rank = row_ref.shape[1]
    rhalf = rank // 2
    rows, cols = snap.shape
    lanes = nz * 64
    per_row = cols // lanes
    chunk = cols // 2
    depth = min(rows, 256)

    loads = []
    for h in range(2):
        cut = pl.ds(h * chunk, chunk)
        load = pltpu.make_async_copy(snap_ref.at[0, :, cut], snap.at[:, cut], load_sem.at[h])
        load.start()
        loads.append(load)

    barrier = pltpu.get_barrier_semaphore()

    def greet(grp, core):
        pl.semaphore_signal(barrier, inc=1, device_id=(grp, core), device_id_type=MESH)

    greet(me, sibling)
    for d in range(1, nz):
        greet(((zi + d) % nz) * nplane + pi, rep)
    for d in range(1, nplane):
        greet(zi * nplane + (pi + d) % nplane, rep)

    def to_core(stage, src, dst):
        copy = pltpu.make_async_remote_copy(
            src_ref=src, dst_ref=dst, send_sem=core_s.at[stage], recv_sem=core_r.at[stage],
            device_id=(me, sibling), device_id_type=MESH)
        copy.start()
        return copy

    def along_z(stage, src, dst):
        copies = []
        for d in range(1, nz):
            q = (zi + d) % nz
            copy = pltpu.make_async_remote_copy(
                src_ref=src(q), dst_ref=dst, send_sem=z_s.at[stage, d], recv_sem=z_r.at[stage, d],
                device_id=(q * nplane + pi, rep), device_id_type=MESH)
            copy.start()
            copies.append(copy)
        return copies

    def in_plane(stage, src, dst):
        copies = []
        for d in range(1, nplane):
            q = (pi + d) % nplane
            copy = pltpu.make_async_remote_copy(
                src_ref=src(q), dst_ref=dst, send_sem=plane_s.at[stage, d], recv_sem=plane_r.at[stage, d],
                device_id=(zi * nplane + q, rep), device_id_type=MESH)
            copy.start()
            copies.append(copy)
        return copies

    started = []

    def arrive(copies):
        for copy in copies:
            copy.wait_recv()
        started.extend(copies)

    uhigh, ulow = split(row_ref[...].T)
    core_copies = []
    for h in range(2):
        loads[h].wait()
        total = jnp.zeros((rank, chunk), F32)
        for k in range(0, rows, depth):
            high, low = split(snap[k:k + depth, h * chunk:(h + 1) * chunk])
            shigh[k:k + depth, h * chunk:(h + 1) * chunk] = high
            slow[k:k + depth, h * chunk:(h + 1) * chunk] = low
            uh, ul = uhigh[:, k:k + depth], ulow[:, k:k + depth]
            total = total + (half(uh, high) + (half(ul, high) + half(uh, low)))
        proj[:, h * chunk:(h + 1) * chunk] = total
        if h == 0:
            pl.semaphore_wait(barrier, nz + nplane - 1)
        cut = pl.ds(h * chunk, chunk)
        core_copies.append(to_core(h, proj.at[pl.ds(sibling * rhalf, rhalf), cut], other.at[:, cut]))
    arrive(core_copies)
    for q in range(nplane):
        at, lo = (q // per_row) * 8, (q % per_row) * lanes
        piece[q] = proj[pl.ds(rep * rhalf + at, 8), lo:lo + lanes] + other[at:at + 8, lo:lo + lanes]

    copies = in_plane(0, lambda q: piece.at[q], plane_in.at[pi])
    plane_in[pi] = piece[pi]
    arrive(copies)
    for t in range(nz // 2):
        for m in range(nplane // 2):
            even, odd = pair(plane_in[2 * m, :, t * 128:(t + 1) * 128], plane_in[2 * m + 1, :, t * 128:(t + 1) * 128])
            zsend[2 * t, m * 8:m * 8 + 8, :] = even
            zsend[2 * t + 1, m * 8:m * 8 + 8, :] = odd
    zrows = nplane * 4
    mine = pl.ds(zi * zrows, zrows)
    copies = along_z(0, lambda q: zsend.at[q], owned.at[mine])
    owned[mine, :] = zsend[zi]
    arrive(copies)
    flat = jnp.concatenate([owned[pl.ds(c, count, stride=4), :] for c in range(4)], axis=1)

    tpart[...] = full(full(time_ref[...], flat), flat, NT)
    swap = to_core(2, tpart, tother)
    arrive([swap])
    tchip[...] = tpart[...] + tother[...]
    trows = tchip.shape[0] // nz
    copies = along_z(1, lambda q: tchip.at[pl.ds(q * trows, trows)], tz.at[zi])
    tz[zi] = tchip[pl.ds(zi * trows, trows), :]
    arrive(copies)
    tsum[...] = functools.reduce(jnp.add, [tz[k] for k in range(nz)])
    copies = in_plane(1, lambda q: tsum, tplane.at[pi])
    tplane[pi] = tsum[...]
    arrive(copies)
    tmine = pl.ds(zi * trows, trows)
    tall[tmine, :] = functools.reduce(jnp.add, [tplane[k] for k in range(nplane)])
    copies = along_z(2, lambda q: tall.at[tmine], tall.at[tmine])
    arrive(copies)
    start = tall[...]

    scale = 1.0 / jnp.sqrt(jnp.sum(start * start, axis=(0, 1), keepdims=True) + 1e-06)

    def time_step(_, basis):
        return 1.5 * basis - 0.5 * full(full(basis, basis, NT), basis)

    basis = lax.fori_loop(0, STEPS, time_step, start * scale)
    time_out[...] = basis * math.sqrt(count)
    mixed = full(full(basis.T, basis), flat)
    for c in range(4):
        wback[pl.ds(c, count, stride=4), :] = mixed[:, c * 128:(c + 1) * 128]

    copies = along_z(3, lambda q: wback.at[pl.ds(q * zrows, zrows)], wz.at[zi])
    wz[zi] = wback[mine, :]
    arrive(copies)
    for t in range(nz // 2):
        for m in range(nplane // 2):
            even, odd = pair(wz[2 * t, m * 8:m * 8 + 8, :], wz[2 * t + 1, m * 8:m * 8 + 8, :])
            wsend[2 * m, :, t * 128:(t + 1) * 128] = even
            wsend[2 * m + 1, :, t * 128:(t + 1) * 128] = odd
    copies = in_plane(2, lambda q: wsend.at[q], wpieces.at[rep, pi])
    wpieces[rep, pi] = wsend[pi]
    arrive(copies)
    swap = to_core(3, wpieces.at[rep], wpieces.at[rep])
    arrive([swap])
    for core in range(2):
        for k in range(rhalf // 16):
            for h in range(per_row):
                block = jnp.concatenate(
                    [wpieces[core, 2 * k * per_row + h], wpieces[core, (2 * k + 1) * per_row + h]], axis=0)
                high, low = split(block)
                at, lo = core * rhalf + k * 16, h * lanes
                whigh[at:at + 16, lo:lo + lanes] = high
                wlow[at:at + 16, lo:lo + lanes] = low

    for k in range(0, rows, depth):
        high, low = shigh[k:k + depth, :], slow[k:k + depth, :]
        prod[k:k + depth, :] = half(high, whigh[...], NT) + (half(high, wlow[...], NT) + half(low, whigh[...], NT))

    prows = rows // nplane
    copies = in_plane(3, lambda q: prod.at[pl.ds(q * prows, prows)], pin.at[pi])
    pin[pi] = prod[pl.ds(pi * prows, prows), :]
    arrive(copies)
    psum[...] = functools.reduce(jnp.add, [pin[k] for k in range(nplane)])
    copies = along_z(4, lambda q: psum.at[pl.ds(q * 8, 8)], pz.at[zi])
    pz[zi] = psum[pl.ds(zi * 8, 8), :]
    arrive(copies)
    xmine = pl.ds(pi * prows + zi * 8, 8)
    xall[xmine, :] = functools.reduce(jnp.add, [pz[k] for k in range(nz)])
    copies = along_z(5, lambda q: xall.at[xmine], xall.at[xmine])
    arrive(copies)
    xplane = pl.ds(pi * prows, prows)
    copies = in_plane(4, lambda q: xall.at[xplane], xall.at[xplane])
    arrive(copies)

    whole = xall[...]
    gpart[...] = full(whole.T, whole)
    swap = to_core(4, gpart, gother)
    arrive([swap])
    gram = gpart[...] + gother[...]
    eye = jnp.where(
        lax.broadcasted_iota(jnp.int32, gram.shape, 0) == lax.broadcasted_iota(jnp.int32, gram.shape, 1), 1.0, 0.0
    ).astype(F32)
    norm = 1.0 / (jnp.sum(gram * eye, axis=(0, 1), keepdims=True) + 1e-06)

    def row_step(_, carry):
        inner, power = carry
        factor = 1.5 * eye - 0.5 * inner
        return full(factor, full(factor, inner)), full(factor, power)

    inner, power = gram * norm, eye
    for k in range(STEPS - 1):
        inner, power = row_step(k, (inner, power))
    power = full(power, 1.5 * eye - 0.5 * inner)
    rows_out[...] = full(whole, power * (math.sqrt(2 * rows) * jnp.sqrt(norm)))
    for copy in started:
        copy.wait_send()


def solution(mesh):
    count = mesh.shape["grp"]
    nz = ZS
    nplane = count // nz

    def on_device(snapshots, row_factor, time_factor):
        _, rows, cols = snapshots.shape
        rank = row_factor.shape[1]
        modes = time_factor.shape[1]
        lanes = nz * 64
        vmem = lambda *shape: pltpu.VMEM(shape, F32)
        narrow = lambda *shape: pltpu.VMEM(shape, BF16)
        sems = lambda *shape: pltpu.SemaphoreType.DMA(shape)
        prows = rows // nplane
        new_rows, new_time = pl.pallas_call(
            functools.partial(kernel, nz),
            out_shape=(
                jax.ShapeDtypeStruct((rows, rank), F32),
                jax.ShapeDtypeStruct((modes, count), F32),
            ),
            in_specs=[
                pl.BlockSpec(memory_space=pltpu.HBM),
                pl.BlockSpec(memory_space=pltpu.VMEM),
                pl.BlockSpec(memory_space=pltpu.VMEM),
            ],
            out_specs=(pl.BlockSpec(memory_space=pltpu.VMEM),) * 2,
            scratch_shapes=[
                vmem(rows, cols), narrow(rows, cols), narrow(rows, cols),
                vmem(rank, cols), vmem(rank // 2, cols),
                vmem(nplane, 8, lanes), vmem(nplane, 8, lanes),
                vmem(nz, nplane * 4, 128), vmem(count * 4, 128),
                vmem(modes, count), vmem(modes, count), vmem(modes, count),
                vmem(nz, modes // nz, count), vmem(modes // nz, count),
                vmem(nplane, modes // nz, count), vmem(modes, count),
                vmem(count * 4, 128), vmem(nz, nplane * 4, 128),
                vmem(nplane, 8, lanes), vmem(2, nplane, 8, lanes),
                narrow(rank, cols), narrow(rank, cols),
                vmem(rows, rank), vmem(nplane, prows, rank), vmem(prows, rank),
                vmem(nz, 8, rank), vmem(rows, rank), vmem(rank, rank), vmem(rank, rank),
                sems(2), sems(5), sems(5), sems(5, nplane), sems(5, nplane), sems(6, nz), sems(6, nz),
            ],
            compiler_params=pltpu.CompilerParams(
                collective_id=0, has_side_effects=True, vmem_limit_bytes=40 * 1024 * 1024),
        )(snapshots, row_factor, time_factor.T)
        return new_rows, new_time.T

    return jax.shard_map(
        on_device,
        mesh=mesh,
        in_specs=(P("grp", "rep", None), P("rep", None), P()),
        out_specs=(P("rep", None), P()),
        check_vma=False,
    )
```

time: 990 us -> 104 us (0.11)
  waiting for transfers between devices: 561 us -> 0 us
  blocking collectives: 336 us -> 0 us
  Pallas kernels: 0 us -> 97.6 us
  matrix products: 46.8 us -> 0 us
  between operations: 16.5 us -> 0.65 us
  starting transfers between devices: 13.9 us -> 0 us
    all_gather x1 -> x0, blocking collectives: 310 us -> none  [on_device(): half_block = lax.all_gather(own_rows, 'grp', axis=0, tiled=True)]
    psum x2 -> x0, waiting for transfers between devices: 266 us -> none  [the longest x1 232 us: on_device(): gram_total = lax.psum(gram_part, ('grp', 'rep'))]
    unnamed x5 -> x0, waiting for transfers between devices: 206 us -> none
    pallas_call x0 -> x1, Pallas kernels: none -> 97.6 us  [on_device(): pl.pallas_call(functools.partial(kernel, nz), out_shape=(jax.ShapeDtypeSt...]
    all_gather x1 -> x0, waiting for transfers between devices: 69.5 us -> none  [on_device(): all_block = lax.all_gather(half_block, 'rep', axis=0, tiled=True)]
    dot_general x38 -> x0, matrix products: 46.8 us -> none  [the longest x36 31.7 us: highdot(): jnp.dot(left, right, precision=lax.Precision.HIGHEST, preferred_element_t...]
    all_to_all x1 -> x0, blocking collectives: 25.9 us -> none  [on_device(): lax.all_to_all(weights, 'grp', split_axis=0, concat_axis=1, tiled=True)]
    all_to_all x1 -> x0, waiting for transfers between devices: 19 us -> none  [on_device(): lax.all_to_all(summed, 'grp', split_axis=1, concat_axis=0, tiled=True)]
  transfers between devices with their start and end apart: 5 -> 0, of which waited for: 5 -> 0; matrix products, arithmetic and copies ran while one was open for 0% -> 0% of each run, Pallas kernels for 0% -> 0%
where the time goes in v1:
time: 104 us
  Pallas kernels  97.6 us (94%)
  local copies, waits for them, and re-layouts  5.39 us (5%)
    pallas_call x1, Pallas kernels, on_device(): pl.pallas_call(functools.partial(kernel, nz), out_shape=(jax.ShapeDtypeSt...  97.6 us
    unnamed x8, local copies, waits for them, and re-layouts  5.39 us

profile of v1, /device:TPU:1, one launch (start us, length us, event | category | flops | bytes accessed | tf_op | source)
XLA Modules:
  0.0 103.7 jit_solution(3373831405942535248)
XLA Ops:
  0.6 0.0 copy-start
  0.6 2.2 %copy-done = f32[1,1024,1024]{2,1,0:T(8,128)S(1)} copy-done((f32[1,1024,1024]{2,1,0:T(8,128)S(1)}, f32[1,1024,1024]{2,1,0:T(8,128)}, u32[]{:S(2)}) %copy-start) | copy-done | bytes 4194328
  2.8 0.0 copy-start.1
  2.8 1.0 %copy-done.1 = f32[1024,128]{1,0:T(8,128)S(1)} copy-done((f32[1024,128]{1,0:T(8,128)S(1)}, f32[1024,128]{1,0:T(8,128)}, u32[]{:S(2)}) %copy-start.1) | copy-done | bytes 524312
  3.9 0.0 copy-start.2
  3.9 0.8 copy-done.2
  4.6 97.6 %shard_map.50 = (f32[1024,128]{1,0:T(8,128)S(1)}, f32[64,128]{1,0:T(8,128)S(1)}) custom-call(f32[1,1024,1024]{2,1,0:T(8,128)S(1)} %copy-done, f32[1024,128]{1,0:T(8,128)S(1)} %copy-done.1, f32[64,128]{1,0:T(8,128)S(1)} %bitcast.2), custom_call_target="tpu_custom_call" | custom-call | tf_op jit(solution)/shard_map/pallas_call | solution.py:261
  102.3 0.8 copy.7
  103.0 0.6 copy.8
Async XLA Ops:
  0.6 2.2 %copy-start = (f32[1,1024,1024]{2,1,0:T(8,128)S(1)}, f32[1,1024,1024]{2,1,0:T(8,128)}, u32[]{:S(2)}) copy-start(f32[1,1024,1024]{2,1,0:T(8,128)} %snap_ref.1) | copy-start | bytes 12582916
  2.8 1.0 %copy-start.1 = (f32[1024,128]{1,0:T(8,128)S(1)}, f32[1024,128]{1,0:T(8,128)}, u32[]{:S(2)}) copy-start(f32[1024,128]{1,0:T(8,128)} %row_ref.1) | copy-start | bytes 1572868
  3.9 0.8 copy-start.2

commit v2 on v0

v2 whole, which is shorter than its diff:
```python
import functools
import math

import jax
import jax.numpy as jnp
from jax import lax
from jax.experimental import pallas as pl
from jax.experimental.pallas import tpu as pltpu
from jax.sharding import PartitionSpec as P

MESH = pl.DeviceIdType.MESH
STEPS = 8
DIMS = (8, 4, 4)
SPREAD = 37
PARTS = 4
VMEM_MIB = 60
F32 = jnp.float32
BF16 = jnp.bfloat16
NN = (((1,), (0,)), ((), ()))
NT = (((1,), (1,)), ((), ()))


def full(left, right, dims=NN):
    return lax.dot_general(left, right, dims, precision=lax.Precision.HIGHEST, preferred_element_type=F32)


def half(left, right, dims=NN):
    return lax.dot_general(left, right, dims, preferred_element_type=F32)


def split(value):
    high = value.astype(BF16)
    return high, (value - high.astype(F32)).astype(BF16)


def kernel(dims, snap_ref, row_ref, time_ref, rows_out, time_out,
           snap, ufac, tfac, shigh, slow, proj, other, piece, owned,
           tpart, tother, tchip, tz, tsum, tplane, tall,
           wback, wpieces, whigh, wlow,
           prod, pin, psum, pz, xall, gpart, gother,
           load_sem, core_s, core_r, plane_s, plane_r, z_s, z_r, all_s, all_r):
    nz, nx, ny = dims
    nplane = nx * ny
    count = nz * nplane
    me = lax.axis_index("grp")
    rep = lax.axis_index("rep")
    zi, pi = me // nplane, me % nplane
    sibling = 1 - rep
    rank = ufac.shape[1]
    rhalf = rank // 2
    rows, cols = snap.shape
    tiles = ny // 2
    width = tiles * 128
    block = nz * ny * 4
    depth = min(rows, 256)

    loads = [pltpu.make_async_copy(row_ref, ufac, load_sem.at[nx]), pltpu.make_async_copy(time_ref, tfac, load_sem.at[nx + 1])]
    for c in range(nx):
        cut = pl.ds(c * width, width)
        loads.append(pltpu.make_async_copy(snap_ref.at[0, :, cut], snap.at[:, cut], load_sem.at[c]))
    for load in loads:
        load.start()

    barrier = pltpu.get_barrier_semaphore()

    def greet(grp, core):
        pl.semaphore_signal(barrier, inc=1, device_id=(grp, core), device_id_type=MESH)

    def greet_one(d, carry):
        greet((me + d * SPREAD) % count, rep)
        return carry

    greet(me, sibling)
    lax.fori_loop(1, count, greet_one, 0)

    started = []

    def begin(copy):
        copy.start()
        started.append(copy)
        return copy

    def to_core(stage, src, dst):
        return [begin(pltpu.make_async_remote_copy(
            src_ref=src, dst_ref=dst, send_sem=core_s.at[stage], recv_sem=core_r.at[stage],
            device_id=(me, sibling), device_id_type=MESH))]

    def along_z(stage, src, dst):
        return [begin(pltpu.make_async_remote_copy(
            src_ref=src, dst_ref=dst, send_sem=z_s.at[stage, d], recv_sem=z_r.at[stage, d],
            device_id=((zi + d) % nz * nplane + pi, rep), device_id_type=MESH)) for d in range(1, nz)]

    def in_plane(stage, src, dst):
        copies = []
        for d in range(1, nplane):
            q = (pi + d) % nplane
            copies.append(begin(pltpu.make_async_remote_copy(
                src_ref=src(q), dst_ref=dst, send_sem=plane_s.at[stage, d], recv_sem=plane_r.at[stage, d],
                device_id=(zi * nplane + q, rep), device_id_type=MESH)))
        return copies

    def arrive(copies):
        for copy in copies:
            copy.wait_recv()

    def place(grp):
        z, x, y = grp // nplane, grp % nplane // ny, grp % ny
        return (x + z) % nx * block + z * (ny * 4) + y * 4

    def to_owner(stage, src, dst, grp):
        return pltpu.make_async_remote_copy(
            src_ref=src, dst_ref=dst, send_sem=all_s.at[stage], recv_sem=all_r.at[stage],
            device_id=(grp, rep), device_id_type=MESH)

    loads[0].wait()
    uhigh, ulow = split(ufac[...].T)
    core_copies = []
    for c in range(nx):
        loads[2 + c].wait()
        lo = c * width
        total = jnp.zeros((rank, width), F32)
        for k in range(0, rows, depth):
            high, low = split(snap[k:k + depth, lo:lo + width])
            shigh[k:k + depth, lo:lo + width] = high
            slow[k:k + depth, lo:lo + width] = low
            uh, ul = uhigh[:, k:k + depth], ulow[:, k:k + depth]
            total = total + (half(uh, high) + (half(ul, high) + half(uh, low)))
        for core in range(2):
            for z in range(nz):
                for k in range(tiles):
                    at = c * block + z * ny * 4 + k * 8
                    proj[core, at:at + 8, :] = total[core * rhalf + z * 8:core * rhalf + z * 8 + 8, k * 128:k * 128 + 128]
        if c == 0:
            pl.semaphore_wait(barrier, count)
        cut = pl.ds(c * block, block)
        core_copies.append(to_core(c, proj.at[sibling, cut], other.at[cut]))

    for c in range(nx):
        arrive(core_copies[c])
        at = c * block
        piece[at:at + block, :] = proj[rep, at:at + block, :] + other[at:at + block, :]

        def send(u, carry):
            v = (u * 5 + zi * ny + pi % ny) % (nz * ny)
            z, y = v // ny, v % ny
            grp = z * nplane + (c + nx * nz - z) % nx * ny + y

            @pl.when(grp != me)
            def _():
                to_owner(0, piece.at[pl.ds(at + z * (ny * 4) + y * 4, 4)], owned.at[pl.ds(me * 4, 4)], grp).start()

            return carry

        lax.fori_loop(0, nz * ny, send, 0)
    pltpu.make_async_copy(piece.at[pl.ds(place(me), 4)], owned.at[pl.ds(me * 4, 4)], all_r.at[0]).start()
    pltpu.make_async_copy(owned, owned, all_r.at[0]).wait()
    flat = jnp.concatenate([owned[pl.ds(c, count, stride=4), :] for c in range(4)], axis=1)

    loads[1].wait()
    tpart[...] = full(full(tfac[...], flat), flat, NT)
    thalf = tpart.shape[0] // 2
    tmine = pl.ds(rep * thalf, thalf)
    arrive(to_core(nx, tpart.at[pl.ds(sibling * thalf, thalf)], tother))
    tchip[...] = tpart[tmine, :] + tother[...]
    copies = along_z(0, tchip, tz.at[zi])
    tz[zi] = tchip[...]
    arrive(copies)
    tsum[...] = functools.reduce(jnp.add, [tz[k] for k in range(nz)])
    copies = in_plane(0, lambda q: tsum, tplane.at[pi])
    tplane[pi] = tsum[...]
    arrive(copies)
    tall[tmine, :] = functools.reduce(jnp.add, [tplane[k] for k in range(nplane)])
    arrive(to_core(nx + 1, tall.at[tmine], tall.at[tmine]))
    start = tall[...]

    scale = 1.0 / jnp.sqrt(jnp.sum(start * start, axis=(0, 1), keepdims=True) + 1e-06)

    def time_step(_, basis):
        return 1.5 * basis - 0.5 * full(full(basis, basis, NT), basis)

    basis = lax.fori_loop(0, STEPS, time_step, start * scale)
    time_out[...] = basis * math.sqrt(count)
    mixed = full(full(basis.T, basis), flat)
    for c in range(4):
        wback[pl.ds(c, count, stride=4), :] = mixed[:, c * 128:(c + 1) * 128]

    spot = pl.ds(place(me), 4)

    def send_back(d, carry):
        grp = (me + d * SPREAD) % count
        to_owner(1, wback.at[pl.ds(grp * 4, 4)], wpieces.at[rep, spot], grp).start()
        return carry

    lax.fori_loop(1, count, send_back, 0)
    pltpu.make_async_copy(wback.at[pl.ds(me * 4, 4)], wpieces.at[rep, spot], all_r.at[1]).start()
    pltpu.make_async_copy(wback, wback, all_r.at[1]).wait()
    arrive(to_core(nx + 2, wpieces.at[rep], wpieces.at[rep]))
    for core in range(2):
        for m in range(nz // 2):
            for c in range(nx):
                for k in range(tiles):
                    at = c * block + 2 * m * ny * 4 + k * 8
                    both = jnp.concatenate(
                        [wpieces[core, at:at + 8, :], wpieces[core, at + ny * 4:at + ny * 4 + 8, :]], axis=0)
                    high, low = split(both)
                    row, lo = core * rhalf + m * 16, c * width + k * 128
                    whigh[row:row + 16, lo:lo + 128] = high
                    wlow[row:row + 16, lo:lo + 128] = low

    part = rows // PARTS
    prows = part // nplane
    summed, crossed, spread = [], [], []
    for h in range(PARTS):
        for k in range(h * part, (h + 1) * part, min(part, 256)):
            high, low = shigh[k:k + min(part, 256), :], slow[k:k + min(part, 256), :]
            prod[k:k + min(part, 256), :] = half(high, whigh[...], NT) + (
                half(high, wlow[...], NT) + half(low, whigh[...], NT))
        summed.append(in_plane(1 + h, lambda q: prod.at[pl.ds(h * part + q * prows, prows)], pin.at[h, pi]))
        pin[h, pi] = prod[pl.ds(h * part + pi * prows, prows), :]
    for h in range(PARTS):
        arrive(summed[h])
        psum[h] = functools.reduce(jnp.add, [pin[h, k] for k in range(nplane)])
        crossed.append(along_z(1 + h, psum.at[h], pz.at[h, zi]))
        pz[h, zi] = psum[h]
    for h in range(PARTS):
        arrive(crossed[h])
        mine = pl.ds(h * part + pi * prows, prows)
        xall[mine, :] = functools.reduce(jnp.add, [pz[h, k] for k in range(nz)])
        spread.append(in_plane(1 + PARTS + h, lambda q: xall.at[mine], xall.at[mine]))
    gram = jnp.zeros((rank, rank), F32)
    for h in range(PARTS):
        arrive(spread[h])
        some = xall[h * part:(h + 1) * part, :]
        gram = gram + full(some.T, some)
    gpart[...] = gram
    arrive(to_core(nx + 3, gpart, gother))
    gram = gpart[...] + gother[...]

    eye = jnp.where(
        lax.broadcasted_iota(jnp.int32, gram.shape, 0) == lax.broadcasted_iota(jnp.int32, gram.shape, 1), 1.0, 0.0
    ).astype(F32)
    norm = 1.0 / (jnp.sum(gram * eye, axis=(0, 1), keepdims=True) + 1e-06)
    inner, power = gram * norm, eye
    for _ in range(STEPS - 1):
        factor = 1.5 * eye - 0.5 * inner
        inner, power = full(factor, full(factor, inner)), full(factor, power)
    power = full(power, 1.5 * eye - 0.5 * inner)
    rows_out[...] = full(xall[...], power * (math.sqrt(2 * rows) * jnp.sqrt(norm)))
    for copy in started:
        copy.wait_send()
    rest = pl.ds(0, (count - 1) * 4)
    for stage in range(2):
        pltpu.make_async_copy(owned.at[rest], owned.at[rest], all_s.at[stage]).wait()


def solution(mesh):
    nz, nx, ny = dims = DIMS
    nplane = nx * ny
    count = nz * nplane

    def on_device(snapshots, row_factor, time_factor):
        _, rows, cols = snapshots.shape
        rank = row_factor.shape[1]
        modes = time_factor.shape[1]
        vmem = lambda *shape: pltpu.VMEM(shape, F32)
        narrow = lambda *shape: pltpu.VMEM(shape, BF16)
        sems = lambda *shape: pltpu.SemaphoreType.DMA(shape)
        part = rows // PARTS
        prows = part // nplane
        new_rows, new_time = pl.pallas_call(
            functools.partial(kernel, dims),
            out_shape=(
                jax.ShapeDtypeStruct((rows, rank), F32),
                jax.ShapeDtypeStruct((modes, count), F32),
            ),
            in_specs=[pl.BlockSpec(memory_space=pltpu.HBM)] * 3,
            out_specs=(pl.BlockSpec(memory_space=pltpu.VMEM),) * 2,
            scratch_shapes=[
                vmem(rows, cols), vmem(rows, rank), vmem(modes, count), narrow(rows, cols), narrow(rows, cols),
                vmem(2, count * 4, 128), vmem(count * 4, 128), vmem(count * 4, 128), vmem(count * 4, 128),
                vmem(modes, count), vmem(modes // 2, count), vmem(modes // 2, count),
                vmem(nz, modes // 2, count), vmem(modes // 2, count),
                vmem(nplane, modes // 2, count), vmem(modes, count),
                vmem(count * 4, 128), vmem(2, count * 4, 128),
                narrow(rank, cols), narrow(rank, cols),
                vmem(rows, rank), vmem(PARTS, nplane, prows, rank), vmem(PARTS, prows, rank),
                vmem(PARTS, nz, prows, rank), vmem(rows, rank), vmem(rank, rank), vmem(rank, rank),
                sems(nx + 2), sems(nx + 4), sems(nx + 4), sems(1 + 2 * PARTS, nplane), sems(1 + 2 * PARTS, nplane),
                sems(1 + PARTS, nz), sems(1 + PARTS, nz), sems(2), sems(2),
            ],
            compiler_params=pltpu.CompilerParams(
                collective_id=0, has_side_effects=True, vmem_limit_bytes=VMEM_MIB * 1024 * 1024),
        )(snapshots, row_factor, time_factor.T)
        return new_rows, new_time.T

    return jax.shard_map(
        on_device,
        mesh=mesh,
        in_specs=(P("grp", "rep", None), P("rep", None), P()),
        out_specs=(P("rep", None), P()),
        check_vma=False,
    )
```

time: 990 us -> 94.8 us (0.10)
  waiting for transfers between devices: 561 us -> 0 us
  blocking collectives: 336 us -> 0 us
  Pallas kernels: 0 us -> 90.7 us
  matrix products: 46.8 us -> 0 us
  between operations: 16.5 us -> 0.64 us
  starting transfers between devices: 13.9 us -> 0 us
    all_gather x1 -> x0, blocking collectives: 310 us -> none  [on_device(): half_block = lax.all_gather(own_rows, 'grp', axis=0, tiled=True)]
    psum x2 -> x0, waiting for transfers between devices: 266 us -> none  [the longest x1 232 us: on_device(): gram_total = lax.psum(gram_part, ('grp', 'rep'))]
    unnamed x5 -> x0, waiting for transfers between devices: 206 us -> none
    pallas_call x0 -> x1, Pallas kernels: none -> 90.7 us  [on_device(): pl.pallas_call(functools.partial(kernel, dims), out_shape=(jax.ShapeDtype...]
    all_gather x1 -> x0, waiting for transfers between devices: 69.5 us -> none  [on_device(): all_block = lax.all_gather(half_block, 'rep', axis=0, tiled=True)]
    dot_general x38 -> x0, matrix products: 46.8 us -> none  [the longest x36 31.7 us: highdot(): jnp.dot(left, right, precision=lax.Precision.HIGHEST, preferred_element_t...]
    all_to_all x1 -> x0, blocking collectives: 25.9 us -> none  [on_device(): lax.all_to_all(weights, 'grp', split_axis=0, concat_axis=1, tiled=True)]
    all_to_all x1 -> x0, waiting for transfers between devices: 19 us -> none  [on_device(): lax.all_to_all(summed, 'grp', split_axis=1, concat_axis=0, tiled=True)]
  transfers between devices with their start and end apart: 5 -> 0, of which waited for: 5 -> 0; matrix products, arithmetic and copies ran while one was open for 0% -> 0% of each run, Pallas kernels for 0% -> 0%
where the time goes in v2:
time: 94.8 us; the launch traced here: 94.6 us
  Pallas kernels  90.7 us (96%)
  local copies, waits for them, and re-layouts  3.24 us (3%)
    pallas_call x1, Pallas kernels, on_device(): pl.pallas_call(functools.partial(kernel, dims), out_shape=(jax.ShapeDtype...  90.7 us
    unnamed x2, local copies, waits for them, and re-layouts  3.24 us

profile of v2, /device:TPU:1, one launch (start us, length us, event | category | flops | bytes accessed | tf_op | source)
XLA Modules:
  0.0 94.6 jit_solution(18370294935484070181)
XLA Ops:
  0.6 90.7 %shard_map.50 = (f32[1024,128]{1,0:T(8,128)}, f32[64,128]{1,0:T(8,128)}) custom-call(f32[1,1024,1024]{2,1,0:T(8,128)} %snap_ref.1, f32[1024,128]{1,0:T(8,128)} %row_ref.1, f32[64,128]{1,0:T(8,128)} %bitcast.2), custom_call_target="tpu_custom_call" | custom-call | tf_op jit(solution)/shard_map/pallas_call | solution.py:270
  91.4 1.9 %copy.7 = f32[1024,128]{1,0:T(8,128)} copy(f32[1024,128]{1,0:T(8,128)} %get-tuple-element.8) | data formatting | bytes 1048576
  93.2 1.4 %copy.8 = f32[128,64]{0,1:T(8,128)} copy(f32[128,64]{0,1:T(8,128)} %bitcast.3) | data formatting | bytes 65536

commit v3 on v2

--- a/solution.py
+++ b/solution.py
@@ -11,9 +11,8 @@
 MESH = pl.DeviceIdType.MESH
 STEPS = 8
 DIMS = (8, 4, 4)
-SPREAD = 37
 PARTS = 4
-VMEM_MIB = 60
+VMEM_MIB = 40
 F32 = jnp.float32
 BF16 = jnp.bfloat16
 NN = (((1,), (0,)), ((), ()))
@@ -35,10 +34,10 @@
 
 def kernel(dims, snap_ref, row_ref, time_ref, rows_out, time_out,
            snap, ufac, tfac, shigh, slow, proj, other, piece, owned,
-           tpart, tother, tchip, tz, tsum, tplane, tall,
+           tpart, tother, tchip, trows, tsum, tall,
            wback, wpieces, whigh, wlow,
            prod, pin, psum, pz, xall, gpart, gother,
-           load_sem, core_s, core_r, plane_s, plane_r, z_s, z_r, all_s, all_r):
+           load_sem, core_s, core_r, plane_s, plane_r, z_s, z_r, all_s, all_r, word_sem):
     nz, nx, ny = dims
     nplane = nx * ny
     count = nz * nplane
@@ -66,12 +65,15 @@
     def greet(grp, core):
         pl.semaphore_signal(barrier, inc=1, device_id=(grp, core), device_id_type=MESH)
 
-    def greet_one(d, carry):
-        greet((me + d * SPREAD) % count, rep)
-        return carry
-
     greet(me, sibling)
-    lax.fori_loop(1, count, greet_one, 0)
+    for d in range(1, nz):
+        greet((zi + d) % nz * nplane + pi, rep)
+    for d in range(1, nplane):
+        greet(zi * nplane + (pi + d) % nplane, rep)
+    pl.semaphore_wait(barrier, nz + nplane - 1)
+    for d in range(1, nz):
+        pl.semaphore_signal(
+            word_sem, inc=1, device_id=((zi + d) % nz * nplane + pi, rep), device_id_type=MESH)
 
     started = []
 
@@ -106,6 +108,11 @@
     def place(grp):
         z, x, y = grp // nplane, grp % nplane // ny, grp % ny
         return (x + z) % nx * block + z * (ny * 4) + y * 4
+
+    def member(c, u):
+        v = (u * 5 + zi * ny + pi % ny) % (nz * ny)
+        z, y = v // ny, v % ny
+        return z * nplane + (c + nx * nz - z) % nx * ny + y, z, y
 
     def to_owner(stage, src, dst, grp):
         return pltpu.make_async_remote_copy(
@@ -130,10 +137,10 @@
                 for k in range(tiles):
                     at = c * block + z * ny * 4 + k * 8
                     proj[core, at:at + 8, :] = total[core * rhalf + z * 8:core * rhalf + z * 8 + 8, k * 128:k * 128 + 128]
-        if c == 0:
-            pl.semaphore_wait(barrier, count)
         cut = pl.ds(c * block, block)
         core_copies.append(to_core(c, proj.at[sibling, cut], other.at[cut]))
+
+    pl.semaphore_wait(word_sem, nz - 1)
 
     for c in range(nx):
         arrive(core_copies[c])
@@ -141,9 +148,7 @@
         piece[at:at + block, :] = proj[rep, at:at + block, :] + other[at:at + block, :]
 
         def send(u, carry):
-            v = (u * 5 + zi * ny + pi % ny) % (nz * ny)
-            z, y = v // ny, v % ny
-            grp = z * nplane + (c + nx * nz - z) % nx * ny + y
+            grp, z, y = member(c, u)
 
             @pl.when(grp != me)
             def _():
@@ -162,14 +167,42 @@
     tmine = pl.ds(rep * thalf, thalf)
     arrive(to_core(nx, tpart.at[pl.ds(sibling * thalf, thalf)], tother))
     tchip[...] = tpart[tmine, :] + tother[...]
-    copies = along_z(0, tchip, tz.at[zi])
-    tz[zi] = tchip[...]
-    arrive(copies)
-    tsum[...] = functools.reduce(jnp.add, [tz[k] for k in range(nz)])
-    copies = in_plane(0, lambda q: tsum, tplane.at[pi])
-    tplane[pi] = tsum[...]
-    arrive(copies)
-    tall[tmine, :] = functools.reduce(jnp.add, [tplane[k] for k in range(nplane)])
+    keeper = (pi // ny + zi) % ny == pi % ny
+    my_row = zi * nx + pi // ny
+
+    def send_row(u, carry):
+        j = (u * 5 + zi * ny + pi % ny) % (nz * nx)
+        z, x = j // nx, j % nx
+        grp = z * nplane + x * ny + (x + z) % ny
+
+        @pl.when(grp != me)
+        def _():
+            to_owner(2, tchip.at[pl.ds(j, 1)], trows.at[pl.ds(me, 1)], grp).start()
+
+        return carry
+
+    lax.fori_loop(0, nz * nx, send_row, 0)
+    spot = pl.ds(rep * thalf + my_row, 1)
+
+    @pl.when(keeper)
+    def _():
+        pltpu.make_async_copy(tchip.at[pl.ds(my_row, 1)], trows.at[pl.ds(me, 1)], all_r.at[2]).start()
+        pltpu.make_async_copy(trows, trows, all_r.at[2]).wait()
+        tsum[...] = jnp.sum(trows[...], axis=0, keepdims=True)
+        for c in range(nx):
+            def send_sum(u, carry):
+                grp, _, _ = member(c, u)
+
+                @pl.when(grp != me)
+                def _():
+                    to_owner(3, tsum, tall.at[spot], grp).start()
+
+                return carry
+
+            lax.fori_loop(0, nz * ny, send_sum, 0)
+        pltpu.make_async_copy(tsum, tall.at[spot], all_r.at[3]).start()
+
+    pltpu.make_async_copy(tchip, tchip, all_r.at[3]).wait()
     arrive(to_core(nx + 1, tall.at[tmine], tall.at[tmine]))
     start = tall[...]
 
@@ -186,12 +219,17 @@
 
     spot = pl.ds(place(me), 4)
 
-    def send_back(d, carry):
-        grp = (me + d * SPREAD) % count
-        to_owner(1, wback.at[pl.ds(grp * 4, 4)], wpieces.at[rep, spot], grp).start()
-        return carry
-
-    lax.fori_loop(1, count, send_back, 0)
+    for c in range(nx):
+        def send_back(u, carry):
+            grp, _, _ = member(c, u)
+
+            @pl.when(grp != me)
+            def _():
+                to_owner(1, wback.at[pl.ds(grp * 4, 4)], wpieces.at[rep, spot], grp).start()
+
+            return carry
+
+        lax.fori_loop(0, nz * ny, send_back, 0)
     pltpu.make_async_copy(wback.at[pl.ds(me * 4, 4)], wpieces.at[rep, spot], all_r.at[1]).start()
     pltpu.make_async_copy(wback, wback, all_r.at[1]).wait()
     arrive(to_core(nx + 2, wpieces.at[rep], wpieces.at[rep]))
@@ -215,18 +253,18 @@
             high, low = shigh[k:k + min(part, 256), :], slow[k:k + min(part, 256), :]
             prod[k:k + min(part, 256), :] = half(high, whigh[...], NT) + (
                 half(high, wlow[...], NT) + half(low, whigh[...], NT))
-        summed.append(in_plane(1 + h, lambda q: prod.at[pl.ds(h * part + q * prows, prows)], pin.at[h, pi]))
+        summed.append(in_plane(h, lambda q: prod.at[pl.ds(h * part + q * prows, prows)], pin.at[h, pi]))
         pin[h, pi] = prod[pl.ds(h * part + pi * prows, prows), :]
     for h in range(PARTS):
         arrive(summed[h])
         psum[h] = functools.reduce(jnp.add, [pin[h, k] for k in range(nplane)])
-        crossed.append(along_z(1 + h, psum.at[h], pz.at[h, zi]))
+        crossed.append(along_z(h, psum.at[h], pz.at[h, zi]))
         pz[h, zi] = psum[h]
     for h in range(PARTS):
         arrive(crossed[h])
         mine = pl.ds(h * part + pi * prows, prows)
         xall[mine, :] = functools.reduce(jnp.add, [pz[h, k] for k in range(nz)])
-        spread.append(in_plane(1 + PARTS + h, lambda q: xall.at[mine], xall.at[mine]))
+        spread.append(in_plane(PARTS + h, lambda q: xall.at[mine], xall.at[mine]))
     gram = jnp.zeros((rank, rank), F32)
     for h in range(PARTS):
         arrive(spread[h])
@@ -251,6 +289,16 @@
     rest = pl.ds(0, (count - 1) * 4)
     for stage in range(2):
         pltpu.make_async_copy(owned.at[rest], owned.at[rest], all_s.at[stage]).wait()
+
+    @pl.when(keeper)
+    def _():
+        less, sent = pl.ds(0, nz * nx - 1), pl.ds(0, count - 1)
+        pltpu.make_async_copy(tchip.at[less], tchip.at[less], all_s.at[2]).wait()
+        pltpu.make_async_copy(trows.at[sent], trows.at[sent], all_s.at[3]).wait()
+
+    @pl.when(jnp.logical_not(keeper))
+    def _():
+        pltpu.make_async_copy(tchip, tchip, all_s.at[2]).wait()
 
 
 def solution(mesh):
@@ -279,18 +327,17 @@
                 vmem(rows, cols), vmem(rows, rank), vmem(modes, count), narrow(rows, cols), narrow(rows, cols),
                 vmem(2, count * 4, 128), vmem(count * 4, 128), vmem(count * 4, 128), vmem(count * 4, 128),
                 vmem(modes, count), vmem(modes // 2, count), vmem(modes // 2, count),
-                vmem(nz, modes // 2, count), vmem(modes // 2, count),
-                vmem(nplane, modes // 2, count), vmem(modes, count),
+                vmem(count, count), vmem(1, count), vmem(modes, count),
                 vmem(count * 4, 128), vmem(2, count * 4, 128),
                 narrow(rank, cols), narrow(rank, cols),
                 vmem(rows, rank), vmem(PARTS, nplane, prows, rank), vmem(PARTS, prows, rank),
                 vmem(PARTS, nz, prows, rank), vmem(rows, rank), vmem(rank, rank), vmem(rank, rank),
-                sems(nx + 2), sems(nx + 4), sems(nx + 4), sems(1 + 2 * PARTS, nplane), sems(1 + 2 * PARTS, nplane),
-                sems(1 + PARTS, nz), sems(1 + PARTS, nz), sems(2), sems(2),
+                sems(nx + 2), sems(nx + 4), sems(nx + 4), sems(2 * PARTS, nplane), sems(2 * PARTS, nplane),
+                sems(PARTS, nz), sems(PARTS, nz), sems(4), sems(4), pltpu.SemaphoreType.REGULAR,
             ],
             compiler_params=pltpu.CompilerParams(
                 collective_id=0, has_side_effects=True, vmem_limit_bytes=VMEM_MIB * 1024 * 1024),
-        )(snapshots, row_factor, time_factor.T)
+        )(*(pltpu.with_memory_space_constraint(arg, pltpu.HBM) for arg in (snapshots, row_factor, time_factor.T)))
         return new_rows, new_time.T
 
     return jax.shard_map(

time: 94.8 us -> 91.2 us (0.962)
  local copies, waits for them, and re-layouts: 3.24 us -> 1.41 us
  Pallas kernels: 90.7 us -> 89 us
    unnamed x2, local copies, waits for them, and re-layouts: 3.24 us -> 1.41 us
    pallas_call x1, Pallas kernels: 90.7 us -> 89 us  [on_device(): pl.pallas_call(functools.partial(kernel, dims), out_shape=(jax.ShapeDtype...]
where the time goes in v3:
time: 91.2 us; the launch traced here: 91.1 us
  Pallas kernels  89 us (98%)
  local copies, waits for them, and re-layouts  1.41 us (2%)
    pallas_call x1, Pallas kernels, on_device(): pl.pallas_call(functools.partial(kernel, dims), out_shape=(jax.ShapeDtype...  89 us

profile of v3, /device:TPU:1, one launch (start us, length us, event | category | flops | bytes accessed | tf_op | source)
XLA Modules:
  0.0 91.1 jit_solution(17505150363856673021)
XLA Ops:
  0.6 89.0 %shard_map.50 = (f32[1024,128]{1,0:T(8,128)S(1)}, f32[64,128]{1,0:T(8,128)S(1)}) custom-call(f32[1,1024,1024]{2,1,0:T(8,128)} %snap_ref.1, f32[1024,128]{1,0:T(8,128)} %row_ref.1, f32[64,128]{1,0:T(8,128)} %bitcast.3), custom_call_target="tpu_custom_call" | custom-call | tf_op jit(solution)/shard_map/pallas_call | solution.py:318
  89.7 0.8 copy.7
  90.5 0.6 copy.8

commit v4 on v2

--- a/solution.py
+++ b/solution.py
@@ -11,9 +11,8 @@
 MESH = pl.DeviceIdType.MESH
 STEPS = 8
 DIMS = (8, 4, 4)
-SPREAD = 37
 PARTS = 4
-VMEM_MIB = 60
+VMEM_MIB = 40
 F32 = jnp.float32
 BF16 = jnp.bfloat16
 NN = (((1,), (0,)), ((), ()))
@@ -33,12 +32,16 @@
     return high, (value - high.astype(F32)).astype(BF16)
 
 
+def far(size):
+    return sorted(range(size), key=lambda d: -min(d, size - d))
+
+
 def kernel(dims, snap_ref, row_ref, time_ref, rows_out, time_out,
            snap, ufac, tfac, shigh, slow, proj, other, piece, owned,
-           tpart, tother, tchip, tz, tsum, tplane, tall,
+           tpart, tz, tsum, tplane, tall,
            wback, wpieces, whigh, wlow,
            prod, pin, psum, pz, xall, gpart, gother,
-           load_sem, core_s, core_r, plane_s, plane_r, z_s, z_r, all_s, all_r):
+           load_sem, core_s, core_r, plane_s, plane_r, z_s, z_r, all_s, all_r, word_sem):
     nz, nx, ny = dims
     nplane = nx * ny
     count = nz * nplane
@@ -66,12 +69,16 @@
     def greet(grp, core):
         pl.semaphore_signal(barrier, inc=1, device_id=(grp, core), device_id_type=MESH)
 
-    def greet_one(d, carry):
-        greet((me + d * SPREAD) % count, rep)
-        return carry
-
     greet(me, sibling)
-    lax.fori_loop(1, count, greet_one, 0)
+    for d in range(1, nz):
+        greet((zi + d) % nz * nplane + pi, rep)
+    for d in range(1, nplane):
+        greet(zi * nplane + (pi + d) % nplane, rep)
+    pl.semaphore_wait(barrier, nz + nplane - 1)
+    for d in range(1, nz):
+        pl.semaphore_signal(
+            word_sem, inc=1, device_id=((zi + d) % nz * nplane + pi, rep), device_id_type=MESH)
+    pl.semaphore_signal(word_sem, inc=1, device_id=(me, sibling), device_id_type=MESH)
 
     started = []
 
@@ -87,7 +94,7 @@
 
     def along_z(stage, src, dst):
         return [begin(pltpu.make_async_remote_copy(
-            src_ref=src, dst_ref=dst, send_sem=z_s.at[stage, d], recv_sem=z_r.at[stage, d],
+            src_ref=src((zi + d) % nz), dst_ref=dst, send_sem=z_s.at[stage, d], recv_sem=z_r.at[stage, d],
             device_id=((zi + d) % nz * nplane + pi, rep), device_id_type=MESH)) for d in range(1, nz)]
 
     def in_plane(stage, src, dst):
@@ -107,10 +114,14 @@
         z, x, y = grp // nplane, grp % nplane // ny, grp % ny
         return (x + z) % nx * block + z * (ny * 4) + y * 4
 
-    def to_owner(stage, src, dst, grp):
+    def to_owner(stage, src, dst, grp, landed=0):
         return pltpu.make_async_remote_copy(
-            src_ref=src, dst_ref=dst, send_sem=all_s.at[stage], recv_sem=all_r.at[stage],
+            src_ref=src, dst_ref=dst, send_sem=all_s.at[stage], recv_sem=all_r.at[landed],
             device_id=(grp, rep), device_id_type=MESH)
+
+    zs = [(zi + d) % nz for d in far(nz)]
+    xs = [(pi // ny + d) % nx for d in far(nx)]
+    ys = [(pi % ny + d) % ny for d in far(ny)]
 
     loads[0].wait()
     uhigh, ulow = split(ufac[...].T)
@@ -130,55 +141,54 @@
                 for k in range(tiles):
                     at = c * block + z * ny * 4 + k * 8
                     proj[core, at:at + 8, :] = total[core * rhalf + z * 8:core * rhalf + z * 8 + 8, k * 128:k * 128 + 128]
-        if c == 0:
-            pl.semaphore_wait(barrier, count)
         cut = pl.ds(c * block, block)
         core_copies.append(to_core(c, proj.at[sibling, cut], other.at[cut]))
+
+    pl.semaphore_wait(word_sem, nz)
 
     for c in range(nx):
         arrive(core_copies[c])
         at = c * block
         piece[at:at + block, :] = proj[rep, at:at + block, :] + other[at:at + block, :]
 
-        def send(u, carry):
-            v = (u * 5 + zi * ny + pi % ny) % (nz * ny)
-            z, y = v // ny, v % ny
-            grp = z * nplane + (c + nx * nz - z) % nx * ny + y
-
-            @pl.when(grp != me)
-            def _():
-                to_owner(0, piece.at[pl.ds(at + z * (ny * 4) + y * 4, 4)], owned.at[pl.ds(me * 4, 4)], grp).start()
-
-            return carry
-
-        lax.fori_loop(0, nz * ny, send, 0)
+        for z in zs:
+            for y in ys:
+                x = (c + nx * nz - z) % nx
+                copy = to_owner(
+                    0, piece.at[pl.ds(at + z * (ny * 4) + y * 4, 4)], owned.at[pl.ds(me * 4, 4)], z * nplane + x * ny + y)
+                if z is zs[-1] and y is ys[-1]:
+                    pl.when(x != pi // ny)(copy.start)
+                else:
+                    copy.start()
     pltpu.make_async_copy(piece.at[pl.ds(place(me), 4)], owned.at[pl.ds(me * 4, 4)], all_r.at[0]).start()
     pltpu.make_async_copy(owned, owned, all_r.at[0]).wait()
     flat = jnp.concatenate([owned[pl.ds(c, count, stride=4), :] for c in range(4)], axis=1)
 
     loads[1].wait()
     tpart[...] = full(full(tfac[...], flat), flat, NT)
-    thalf = tpart.shape[0] // 2
-    tmine = pl.ds(rep * thalf, thalf)
-    arrive(to_core(nx, tpart.at[pl.ds(sibling * thalf, thalf)], tother))
-    tchip[...] = tpart[tmine, :] + tother[...]
-    copies = along_z(0, tchip, tz.at[zi])
-    tz[zi] = tchip[...]
+    trows = tpart.shape[0] // nz
+    copies = along_z(PARTS, lambda q: tpart.at[pl.ds(q * trows, trows)], tz.at[zi])
+    tz[zi] = tpart[pl.ds(zi * trows, trows), :]
     arrive(copies)
     tsum[...] = functools.reduce(jnp.add, [tz[k] for k in range(nz)])
-    copies = in_plane(0, lambda q: tsum, tplane.at[pi])
-    tplane[pi] = tsum[...]
+    copies = in_plane(2 * PARTS, lambda q: tsum, tplane.at[rep, pi])
+    for d in range(nplane):
+        copies.append(begin(pltpu.make_async_remote_copy(
+            src_ref=tsum, dst_ref=tplane.at[rep, pi], send_sem=plane_s.at[2 * PARTS + 1, d],
+            recv_sem=plane_r.at[2 * PARTS + 1, d], device_id=(zi * nplane + (pi + d) % nplane, sibling),
+            device_id_type=MESH)))
+    tplane[rep, pi] = tsum[...]
     arrive(copies)
-    tall[tmine, :] = functools.reduce(jnp.add, [tplane[k] for k in range(nplane)])
-    arrive(to_core(nx + 1, tall.at[tmine], tall.at[tmine]))
+    tmine = pl.ds(zi * trows, trows)
+    tall[tmine, :] = functools.reduce(jnp.add, [tplane[core, k] for core in range(2) for k in range(nplane)])
+    arrive(along_z(PARTS + 1, lambda q: tall.at[tmine], tall.at[tmine]))
     start = tall[...]
 
     scale = 1.0 / jnp.sqrt(jnp.sum(start * start, axis=(0, 1), keepdims=True) + 1e-06)
 
-    def time_step(_, basis):
-        return 1.5 * basis - 0.5 * full(full(basis, basis, NT), basis)
-
-    basis = lax.fori_loop(0, STEPS, time_step, start * scale)
+    basis = start * scale
+    for _ in range(STEPS):
+        basis = 1.5 * basis - 0.5 * full(full(basis, basis, NT), basis)
     time_out[...] = basis * math.sqrt(count)
     mixed = full(full(basis.T, basis), flat)
     for c in range(4):
@@ -186,26 +196,36 @@
 
     spot = pl.ds(place(me), 4)
 
-    def send_back(d, carry):
-        grp = (me + d * SPREAD) % count
-        to_owner(1, wback.at[pl.ds(grp * 4, 4)], wpieces.at[rep, spot], grp).start()
-        return carry
-
-    lax.fori_loop(1, count, send_back, 0)
-    pltpu.make_async_copy(wback.at[pl.ds(me * 4, 4)], wpieces.at[rep, spot], all_r.at[1]).start()
-    pltpu.make_async_copy(wback, wback, all_r.at[1]).wait()
-    arrive(to_core(nx + 2, wpieces.at[rep], wpieces.at[rep]))
-    for core in range(2):
+    my_part = (pi // ny + zi) % nx
+    for z in zs:
+        for x in xs:
+            for y in ys:
+                if not (z is zs[-1] and x is xs[-1] and y is ys[-1]):
+                    grp = z * nplane + x * ny + y
+                    to_owner(1, wback.at[pl.ds(grp * 4, 4)], wpieces.at[rep, spot], grp, 1 + my_part).start()
+    pltpu.make_async_copy(wback.at[pl.ds(me * 4, 4)], wpieces.at[rep, spot], all_r.at[1 + my_part]).start()
+    passed = []
+    for c in range(nx):
+        cut = pl.ds(c * block, block)
+        pltpu.make_async_copy(wback.at[cut], wpieces.at[rep, cut], all_r.at[1 + c]).wait()
+        passed.append(to_core(nx + c, wpieces.at[rep, cut], wpieces.at[rep, cut]))
+
+    def narrowed(core, c):
         for m in range(nz // 2):
-            for c in range(nx):
-                for k in range(tiles):
-                    at = c * block + 2 * m * ny * 4 + k * 8
-                    both = jnp.concatenate(
-                        [wpieces[core, at:at + 8, :], wpieces[core, at + ny * 4:at + ny * 4 + 8, :]], axis=0)
-                    high, low = split(both)
-                    row, lo = core * rhalf + m * 16, c * width + k * 128
-                    whigh[row:row + 16, lo:lo + 128] = high
-                    wlow[row:row + 16, lo:lo + 128] = low
+            for k in range(tiles):
+                at = c * block + 2 * m * ny * 4 + k * 8
+                both = jnp.concatenate(
+                    [wpieces[core, at:at + 8, :], wpieces[core, at + ny * 4:at + ny * 4 + 8, :]], axis=0)
+                high, low = split(both)
+                row, lo = pl.ds(pl.multiple_of(core * rhalf + m * 16, 16), 16), c * width + k * 128
+                whigh[row, lo:lo + 128] = high
+                wlow[row, lo:lo + 128] = low
+
+    for c in range(nx):
+        narrowed(rep, c)
+    for c in range(nx):
+        arrive(passed[c])
+        narrowed(sibling, c)
 
     part = rows // PARTS
     prows = part // nplane
@@ -215,25 +235,25 @@
             high, low = shigh[k:k + min(part, 256), :], slow[k:k + min(part, 256), :]
             prod[k:k + min(part, 256), :] = half(high, whigh[...], NT) + (
                 half(high, wlow[...], NT) + half(low, whigh[...], NT))
-        summed.append(in_plane(1 + h, lambda q: prod.at[pl.ds(h * part + q * prows, prows)], pin.at[h, pi]))
+        summed.append(in_plane(h, lambda q: prod.at[pl.ds(h * part + q * prows, prows)], pin.at[h, pi]))
         pin[h, pi] = prod[pl.ds(h * part + pi * prows, prows), :]
     for h in range(PARTS):
         arrive(summed[h])
         psum[h] = functools.reduce(jnp.add, [pin[h, k] for k in range(nplane)])
-        crossed.append(along_z(1 + h, psum.at[h], pz.at[h, zi]))
+        crossed.append(along_z(h, lambda q: psum.at[h], pz.at[h, zi]))
         pz[h, zi] = psum[h]
     for h in range(PARTS):
         arrive(crossed[h])
         mine = pl.ds(h * part + pi * prows, prows)
         xall[mine, :] = functools.reduce(jnp.add, [pz[h, k] for k in range(nz)])
-        spread.append(in_plane(1 + PARTS + h, lambda q: xall.at[mine], xall.at[mine]))
+        spread.append(in_plane(PARTS + h, lambda q: xall.at[mine], xall.at[mine]))
     gram = jnp.zeros((rank, rank), F32)
     for h in range(PARTS):
         arrive(spread[h])
         some = xall[h * part:(h + 1) * part, :]
         gram = gram + full(some.T, some)
     gpart[...] = gram
-    arrive(to_core(nx + 3, gpart, gother))
+    arrive(to_core(2 * nx, gpart, gother))
     gram = gpart[...] + gother[...]
 
     eye = jnp.where(
@@ -278,19 +298,18 @@
             scratch_shapes=[
                 vmem(rows, cols), vmem(rows, rank), vmem(modes, count), narrow(rows, cols), narrow(rows, cols),
                 vmem(2, count * 4, 128), vmem(count * 4, 128), vmem(count * 4, 128), vmem(count * 4, 128),
-                vmem(modes, count), vmem(modes // 2, count), vmem(modes // 2, count),
-                vmem(nz, modes // 2, count), vmem(modes // 2, count),
-                vmem(nplane, modes // 2, count), vmem(modes, count),
+                vmem(modes, count), vmem(nz, modes // nz, count), vmem(modes // nz, count),
+                vmem(2, nplane, modes // nz, count), vmem(modes, count),
                 vmem(count * 4, 128), vmem(2, count * 4, 128),
                 narrow(rank, cols), narrow(rank, cols),
                 vmem(rows, rank), vmem(PARTS, nplane, prows, rank), vmem(PARTS, prows, rank),
                 vmem(PARTS, nz, prows, rank), vmem(rows, rank), vmem(rank, rank), vmem(rank, rank),
-                sems(nx + 2), sems(nx + 4), sems(nx + 4), sems(1 + 2 * PARTS, nplane), sems(1 + 2 * PARTS, nplane),
-                sems(1 + PARTS, nz), sems(1 + PARTS, nz), sems(2), sems(2),
+                sems(nx + 2), sems(2 * nx + 1), sems(2 * nx + 1), sems(2 * PARTS + 2, nplane), sems(2 * PARTS + 2, nplane),
+                sems(PARTS + 2, nz), sems(PARTS + 2, nz), sems(2), sems(1 + nx), pltpu.SemaphoreType.REGULAR,
             ],
             compiler_params=pltpu.CompilerParams(
                 collective_id=0, has_side_effects=True, vmem_limit_bytes=VMEM_MIB * 1024 * 1024),
-        )(snapshots, row_factor, time_factor.T)
+        )(*(pltpu.with_memory_space_constraint(arg, pltpu.HBM) for arg in (snapshots, row_factor, time_factor.T)))
         return new_rows, new_time.T
 
     return jax.shard_map(

time: 94.8 us -> 86.4 us (0.911)
  Pallas kernels: 90.7 us -> 84.3 us
  local copies, waits for them, and re-layouts: 3.24 us -> 1.41 us
    pallas_call x1, Pallas kernels: 90.7 us -> 84.3 us  [on_device(): pl.pallas_call(functools.partial(kernel, dims), out_shape=(jax.ShapeDtype...]
    unnamed x2, local copies, waits for them, and re-layouts: 3.24 us -> 1.41 us
where the time goes in v4:
time: 86.4 us; the launch traced here: 86.3 us
  Pallas kernels  84.3 us (98%)
  local copies, waits for them, and re-layouts  1.41 us (2%)
    pallas_call x1, Pallas kernels, on_device(): pl.pallas_call(functools.partial(kernel, dims), out_shape=(jax.ShapeDtype...  84.3 us

profile of v4, /device:TPU:1, one launch (start us, length us, event | category | flops | bytes accessed | tf_op | source)
XLA Modules:
  0.0 86.3 jit_solution(6938352696720256704)
XLA Ops:
  0.6 84.3 %shard_map.50 = (f32[1024,128]{1,0:T(8,128)S(1)}, f32[64,128]{1,0:T(8,128)S(1)}) custom-call(f32[1,1024,1024]{2,1,0:T(8,128)} %snap_ref.1, f32[1024,128]{1,0:T(8,128)} %row_ref.1, f32[64,128]{1,0:T(8,128)} %bitcast.3), custom_call_target="tpu_custom_call" | custom-call | tf_op jit(solution)/shard_map/pallas_call | solution.py:290
  84.9 0.8 copy.7
  85.7 0.6 copy.8

commit v5 on v4

--- a/solution.py
+++ b/solution.py
@@ -39,7 +39,7 @@
 def kernel(dims, snap_ref, row_ref, time_ref, rows_out, time_out,
            snap, ufac, tfac, shigh, slow, proj, other, piece, owned,
            tpart, tz, tsum, tplane, tall,
-           wback, wpieces, whigh, wlow,
+           wback, wpieces, wcut,
            prod, pin, psum, pz, xall, gpart, gother,
            load_sem, core_s, core_r, plane_s, plane_r, z_s, z_r, all_s, all_r, word_sem):
     nz, nx, ny = dims
@@ -80,6 +80,9 @@
             word_sem, inc=1, device_id=((zi + d) % nz * nplane + pi, rep), device_id_type=MESH)
     pl.semaphore_signal(word_sem, inc=1, device_id=(me, sibling), device_id_type=MESH)
 
+    ring = sorted(
+        ((dx, dy) for dx in range(nx) for dy in range(ny)),
+        key=lambda at: -min(at[0], nx - at[0]) - min(at[1], ny - at[1]))
     started = []
 
     def begin(copy):
@@ -95,14 +98,15 @@
     def along_z(stage, src, dst):
         return [begin(pltpu.make_async_remote_copy(
             src_ref=src((zi + d) % nz), dst_ref=dst, send_sem=z_s.at[stage, d], recv_sem=z_r.at[stage, d],
-            device_id=((zi + d) % nz * nplane + pi, rep), device_id_type=MESH)) for d in range(1, nz)]
+            device_id=((zi + d) % nz * nplane + pi, rep), device_id_type=MESH)) for d in far(nz)[:-1]]
 
     def in_plane(stage, src, dst):
         copies = []
-        for d in range(1, nplane):
-            q = (pi + d) % nplane
+        for dx, dy in ring[:-1]:
+            q = (pi // ny + dx) % nx * ny + (pi % ny + dy) % ny
             copies.append(begin(pltpu.make_async_remote_copy(
-                src_ref=src(q), dst_ref=dst, send_sem=plane_s.at[stage, d], recv_sem=plane_r.at[stage, d],
+                src_ref=src(q), dst_ref=dst, send_sem=plane_s.at[stage, dx * ny + dy],
+                recv_sem=plane_r.at[stage, dx * ny + dy],
                 device_id=(zi * nplane + q, rep), device_id_type=MESH)))
         return copies
 
@@ -124,7 +128,7 @@
     ys = [(pi % ny + d) % ny for d in far(ny)]
 
     loads[0].wait()
-    uhigh, ulow = split(ufac[...].T)
+    ucut = jnp.concatenate(split(ufac[...].T), axis=0)
     core_copies = []
     for c in range(nx):
         loads[2 + c].wait()
@@ -134,8 +138,8 @@
             high, low = split(snap[k:k + depth, lo:lo + width])
             shigh[k:k + depth, lo:lo + width] = high
             slow[k:k + depth, lo:lo + width] = low
-            uh, ul = uhigh[:, k:k + depth], ulow[:, k:k + depth]
-            total = total + (half(uh, high) + (half(ul, high) + half(uh, low)))
+            first = half(ucut[:, k:k + depth], high)
+            total = total + (first[:rank] + (first[rank:] + half(ucut[:rank, k:k + depth], low)))
         for core in range(2):
             for z in range(nz):
                 for k in range(tiles):
@@ -172,10 +176,11 @@
     arrive(copies)
     tsum[...] = functools.reduce(jnp.add, [tz[k] for k in range(nz)])
     copies = in_plane(2 * PARTS, lambda q: tsum, tplane.at[rep, pi])
-    for d in range(nplane):
+    for dx, dy in ring:
+        q = (pi // ny + dx) % nx * ny + (pi % ny + dy) % ny
         copies.append(begin(pltpu.make_async_remote_copy(
-            src_ref=tsum, dst_ref=tplane.at[rep, pi], send_sem=plane_s.at[2 * PARTS + 1, d],
-            recv_sem=plane_r.at[2 * PARTS + 1, d], device_id=(zi * nplane + (pi + d) % nplane, sibling),
+            src_ref=tsum, dst_ref=tplane.at[rep, pi], send_sem=plane_s.at[2 * PARTS + 1, dx * ny + dy],
+            recv_sem=plane_r.at[2 * PARTS + 1, dx * ny + dy], device_id=(zi * nplane + q, sibling),
             device_id_type=MESH)))
     tplane[rep, pi] = tsum[...]
     arrive(copies)
@@ -218,8 +223,8 @@
                     [wpieces[core, at:at + 8, :], wpieces[core, at + ny * 4:at + ny * 4 + 8, :]], axis=0)
                 high, low = split(both)
                 row, lo = pl.ds(pl.multiple_of(core * rhalf + m * 16, 16), 16), c * width + k * 128
-                whigh[row, lo:lo + 128] = high
-                wlow[row, lo:lo + 128] = low
+                wcut[row, lo:lo + 128] = high
+                wcut[pl.ds(pl.multiple_of(rank + core * rhalf + m * 16, 16), 16), lo:lo + 128] = low
 
     for c in range(nx):
         narrowed(rep, c)
@@ -233,8 +238,8 @@
     for h in range(PARTS):
         for k in range(h * part, (h + 1) * part, min(part, 256)):
             high, low = shigh[k:k + min(part, 256), :], slow[k:k + min(part, 256), :]
-            prod[k:k + min(part, 256), :] = half(high, whigh[...], NT) + (
-                half(high, wlow[...], NT) + half(low, whigh[...], NT))
+            first = half(high, wcut[...], NT)
+            prod[k:k + min(part, 256), :] = first[:, :rank] + (first[:, rank:] + half(low, wcut[:rank, :], NT))
         summed.append(in_plane(h, lambda q: prod.at[pl.ds(h * part + q * prows, prows)], pin.at[h, pi]))
         pin[h, pi] = prod[pl.ds(h * part + pi * prows, prows), :]
     for h in range(PARTS):
@@ -301,7 +306,7 @@
                 vmem(modes, count), vmem(nz, modes // nz, count), vmem(modes // nz, count),
                 vmem(2, nplane, modes // nz, count), vmem(modes, count),
                 vmem(count * 4, 128), vmem(2, count * 4, 128),
-                narrow(rank, cols), narrow(rank, cols),
+                narrow(2 * rank, cols),
                 vmem(rows, rank), vmem(PARTS, nplane, prows, rank), vmem(PARTS, prows, rank),
                 vmem(PARTS, nz, prows, rank), vmem(rows, rank), vmem(rank, rank), vmem(rank, rank),
                 sems(nx + 2), sems(2 * nx + 1), sems(2 * nx + 1), sems(2 * PARTS + 2, nplane), sems(2 * PARTS + 2, nplane),

time: 86.4 us -> 83.6 us (0.968)
  Pallas kernels: 84.3 us -> 81.5 us
    pallas_call x1, Pallas kernels: 84.3 us -> 81.5 us  [on_device(): pl.pallas_call(functools.partial(kernel, dims), out_shape=(jax.ShapeDtype...]
where the time goes in v5:
time: 83.6 us
  Pallas kernels  81.5 us (97%)
  local copies, waits for them, and re-layouts  1.41 us (2%)
    pallas_call x1, Pallas kernels, on_device(): pl.pallas_call(functools.partial(kernel, dims), out_shape=(jax.ShapeDtype...  81.5 us

profile of v5, /device:TPU:1, one launch (start us, length us, event | category | flops | bytes accessed | tf_op | source)
XLA Modules:
  0.0 83.6 jit_solution(1707654749610569401)
XLA Ops:
  0.6 81.5 %shard_map.50 = (f32[1024,128]{1,0:T(8,128)S(1)}, f32[64,128]{1,0:T(8,128)S(1)}) custom-call(f32[1,1024,1024]{2,1,0:T(8,128)} %snap_ref.1, f32[1024,128]{1,0:T(8,128)} %row_ref.1, f32[64,128]{1,0:T(8,128)} %bitcast.3), custom_call_target="tpu_custom_call" | custom-call | tf_op jit(solution)/shard_map/pallas_call | solution.py:295
  82.2 0.8 copy.7
  83.0 0.6 copy.8

commit v6 on v5

--- a/solution.py
+++ b/solution.py
@@ -30,6 +30,30 @@
 def split(value):
     high = value.astype(BF16)
     return high, (value - high.astype(F32)).astype(BF16)
+
+
+def thirds(value):
+    high, rest = value.astype(BF16), value
+    rest = rest - high.astype(F32)
+    mid = rest.astype(BF16)
+    return high, mid, (rest - mid.astype(F32)).astype(BF16)
+
+
+def beside(*blocks):
+    return jnp.concatenate(blocks, axis=1)
+
+
+def above(*blocks):
+    return jnp.concatenate(blocks, axis=0)
+
+
+def six(left, right):
+    high, mid, low = left
+    rhigh, rmid, rlow = right
+    n = rhigh.shape[1]
+    four = half(beside(high, mid), above(beside(rhigh, rmid), beside(rmid, rhigh)))
+    two = half(beside(high, low), above(rlow, rhigh))
+    return four[:, :n] + (four[:, n:] + two)
 
 
 def far(size):
@@ -268,7 +292,9 @@
     inner, power = gram * norm, eye
     for _ in range(STEPS - 1):
         factor = 1.5 * eye - 0.5 * inner
-        inner, power = full(factor, full(factor, inner)), full(factor, power)
+        cut = thirds(factor)
+        power = six(cut, thirds(power))
+        inner = six(cut, thirds(six(cut, thirds(inner))))
     power = full(power, 1.5 * eye - 0.5 * inner)
     rows_out[...] = full(xall[...], power * (math.sqrt(2 * rows) * jnp.sqrt(norm)))
     for copy in started:

time: 83.6 us -> 83.2 us (level)
  no operation moved by 1% of the time
where the time goes in v6:
time: 83.2 us
  Pallas kernels  81.1 us (97%)
  local copies, waits for them, and re-layouts  1.41 us (2%)
    pallas_call x1, Pallas kernels, on_device(): pl.pallas_call(functools.partial(kernel, dims), out_shape=(jax.ShapeDtype...  81.1 us

profile of v6, /device:TPU:1, one launch (start us, length us, event | category | flops | bytes accessed | tf_op | source)
XLA Modules:
  0.0 83.2 jit_solution(10603362366107637411)
XLA Ops:
  0.6 81.1 %shard_map.50 = (f32[1024,128]{1,0:T(8,128)S(1)}, f32[64,128]{1,0:T(8,128)S(1)}) custom-call(f32[1,1024,1024]{2,1,0:T(8,128)} %snap_ref.1, f32[1024,128]{1,0:T(8,128)} %row_ref.1, f32[64,128]{1,0:T(8,128)} %bitcast.3), custom_call_target="tpu_custom_call" | custom-call | tf_op jit(solution)/shard_map/pallas_call | solution.py:321
  81.7 0.8 copy.7
  82.5 0.6 copy.8

commit v7 on v6

--- a/solution.py
+++ b/solution.py
@@ -65,7 +65,7 @@
            tpart, tz, tsum, tplane, tall,
            wback, wpieces, wcut,
            prod, pin, psum, pz, xall, gpart, gother,
-           load_sem, core_s, core_r, plane_s, plane_r, z_s, z_r, all_s, all_r, word_sem):
+           load_sem, core_s, core_r, plane_s, plane_r, z_s, z_r, all_s, all_r, team_s, team_r, sheet_s, sheet_r, word_sem):
     nz, nx, ny = dims
     nplane = nx * ny
     count = nz * nplane
@@ -194,23 +194,41 @@
 
     loads[1].wait()
     tpart[...] = full(full(tfac[...], flat), flat, NT)
-    trows = tpart.shape[0] // nz
-    copies = along_z(PARTS, lambda q: tpart.at[pl.ds(q * trows, trows)], tz.at[zi])
-    tz[zi] = tpart[pl.ds(zi * trows, trows), :]
+    team = 2 * nx
+    trows = tpart.shape[0] // team
+    xi, yi = pi // ny, pi % ny
+    mine = rep * nx + xi
+
+    def in_team(stage, src, dst):
+        copies = []
+        for d in far(nx):
+            for flip in (1, 0):
+                if d or flip:
+                    x, core = (xi + d) % nx, (sibling if flip else rep)
+                    copies.append(begin(pltpu.make_async_remote_copy(
+                        src_ref=src(core * nx + x), dst_ref=dst, send_sem=team_s.at[stage, flip * nx + d],
+                        recv_sem=team_r.at[stage, flip * nx + d],
+                        device_id=(zi * nplane + x * ny + yi, core), device_id_type=MESH)))
+        return copies
+
+    copies = in_team(0, lambda q: tpart.at[pl.ds(q * trows, trows)], tz.at[mine])
+    tz[mine] = tpart[pl.ds(mine * trows, trows), :]
     arrive(copies)
-    tsum[...] = functools.reduce(jnp.add, [tz[k] for k in range(nz)])
-    copies = in_plane(2 * PARTS, lambda q: tsum, tplane.at[rep, pi])
-    for dx, dy in ring:
-        q = (pi // ny + dx) % nx * ny + (pi % ny + dy) % ny
+    tsum[...] = functools.reduce(jnp.add, [tz[k] for k in range(team)])
+    copies = []
+    sheet = sorted(
+        ((dz, dy) for dz in range(nz) for dy in range(ny)),
+        key=lambda at: -min(at[0], nz - at[0]) - min(at[1], ny - at[1]))
+    for dz, dy in sheet[:-1]:
         copies.append(begin(pltpu.make_async_remote_copy(
-            src_ref=tsum, dst_ref=tplane.at[rep, pi], send_sem=plane_s.at[2 * PARTS + 1, dx * ny + dy],
-            recv_sem=plane_r.at[2 * PARTS + 1, dx * ny + dy], device_id=(zi * nplane + q, sibling),
-            device_id_type=MESH)))
-    tplane[rep, pi] = tsum[...]
+            src_ref=tsum, dst_ref=tplane.at[zi * ny + yi], send_sem=sheet_s.at[dz * ny + dy],
+            recv_sem=sheet_r.at[dz * ny + dy],
+            device_id=((zi + dz) % nz * nplane + xi * ny + (yi + dy) % ny, rep), device_id_type=MESH)))
+    tplane[zi * ny + yi] = tsum[...]
     arrive(copies)
-    tmine = pl.ds(zi * trows, trows)
-    tall[tmine, :] = functools.reduce(jnp.add, [tplane[core, k] for core in range(2) for k in range(nplane)])
-    arrive(along_z(PARTS + 1, lambda q: tall.at[tmine], tall.at[tmine]))
+    tmine = pl.ds(mine * trows, trows)
+    tall[tmine, :] = functools.reduce(jnp.add, [tplane[k] for k in range(nz * ny)])
+    arrive(in_team(1, lambda q: tall.at[tmine], tall.at[tmine]))
     start = tall[...]
 
     scale = 1.0 / jnp.sqrt(jnp.sum(start * start, axis=(0, 1), keepdims=True) + 1e-06)
@@ -329,14 +347,15 @@
             scratch_shapes=[
                 vmem(rows, cols), vmem(rows, rank), vmem(modes, count), narrow(rows, cols), narrow(rows, cols),
                 vmem(2, count * 4, 128), vmem(count * 4, 128), vmem(count * 4, 128), vmem(count * 4, 128),
-                vmem(modes, count), vmem(nz, modes // nz, count), vmem(modes // nz, count),
-                vmem(2, nplane, modes // nz, count), vmem(modes, count),
+                vmem(modes, count), vmem(2 * nx, modes // (2 * nx), count), vmem(modes // (2 * nx), count),
+                vmem(nz * ny, modes // (2 * nx), count), vmem(modes, count),
                 vmem(count * 4, 128), vmem(2, count * 4, 128),
                 narrow(2 * rank, cols),
                 vmem(rows, rank), vmem(PARTS, nplane, prows, rank), vmem(PARTS, prows, rank),
                 vmem(PARTS, nz, prows, rank), vmem(rows, rank), vmem(rank, rank), vmem(rank, rank),
-                sems(nx + 2), sems(2 * nx + 1), sems(2 * nx + 1), sems(2 * PARTS + 2, nplane), sems(2 * PARTS + 2, nplane),
-                sems(PARTS + 2, nz), sems(PARTS + 2, nz), sems(2), sems(1 + nx), pltpu.SemaphoreType.REGULAR,
+                sems(nx + 2), sems(2 * nx + 1), sems(2 * nx + 1), sems(2 * PARTS, nplane), sems(2 * PARTS, nplane),
+                sems(PARTS, nz), sems(PARTS, nz), sems(2), sems(1 + nx),
+                sems(2, 2 * nx), sems(2, 2 * nx), sems(nz * ny), sems(nz * ny), pltpu.SemaphoreType.REGULAR,
             ],
             compiler_params=pltpu.CompilerParams(
                 collective_id=0, has_side_effects=True, vmem_limit_bytes=VMEM_MIB * 1024 * 1024),

time: 83.2 us -> 83 us (level)
  no operation moved by 1% of the time
where the time goes in v7:
time: 83 us; the launch traced here: 82.9 us
  Pallas kernels  80.9 us (97%)
  local copies, waits for them, and re-layouts  1.41 us (2%)
    pallas_call x1, Pallas kernels, on_device(): pl.pallas_call(functools.partial(kernel, dims), out_shape=(jax.ShapeDtype...  80.9 us

profile of v7, /device:TPU:1, one launch (start us, length us, event | category | flops | bytes accessed | tf_op | source)
XLA Modules:
  0.0 82.9 jit_solution(9824622723688295487)
XLA Ops:
  0.6 80.9 %shard_map.50 = (f32[1024,128]{1,0:T(8,128)S(1)}, f32[64,128]{1,0:T(8,128)S(1)}) custom-call(f32[1,1024,1024]{2,1,0:T(8,128)} %snap_ref.1, f32[1024,128]{1,0:T(8,128)} %row_ref.1, f32[64,128]{1,0:T(8,128)} %bitcast.3), custom_call_target="tpu_custom_call" | custom-call | tf_op jit(solution)/shard_map/pallas_call | solution.py:339
  81.5 0.8 copy.7
  82.3 0.6 copy.8

commit v8 on v7

--- a/solution.py
+++ b/solution.py
@@ -277,6 +277,7 @@
     part = rows // PARTS
     prows = part // nplane
     summed, crossed, spread = [], [], []
+    early = list(started)
     for h in range(PARTS):
         for k in range(h * part, (h + 1) * part, min(part, 256)):
             high, low = shigh[k:k + min(part, 256), :], slow[k:k + min(part, 256), :]
@@ -294,13 +295,22 @@
         mine = pl.ds(h * part + pi * prows, prows)
         xall[mine, :] = functools.reduce(jnp.add, [pz[h, k] for k in range(nz)])
         spread.append(in_plane(PARTS + h, lambda q: xall.at[mine], xall.at[mine]))
+    for copy in early + [copy for copies in summed + crossed for copy in copies]:
+        copy.wait_send()
+    rest = pl.ds(0, (count - 1) * 4)
+    for stage in range(2):
+        pltpu.make_async_copy(owned.at[rest], owned.at[rest], all_s.at[stage]).wait()
     gram = jnp.zeros((rank, rank), F32)
     for h in range(PARTS):
         arrive(spread[h])
         some = xall[h * part:(h + 1) * part, :]
         gram = gram + full(some.T, some)
     gpart[...] = gram
-    arrive(to_core(2 * nx, gpart, gother))
+    swap = to_core(2 * nx, gpart, gother)
+    for copies in spread:
+        for copy in copies:
+            copy.wait_send()
+    arrive(swap)
     gram = gpart[...] + gother[...]
 
     eye = jnp.where(
@@ -315,11 +325,8 @@
         inner = six(cut, thirds(six(cut, thirds(inner))))
     power = full(power, 1.5 * eye - 0.5 * inner)
     rows_out[...] = full(xall[...], power * (math.sqrt(2 * rows) * jnp.sqrt(norm)))
-    for copy in started:
+    for copy in swap:
         copy.wait_send()
-    rest = pl.ds(0, (count - 1) * 4)
-    for stage in range(2):
-        pltpu.make_async_copy(owned.at[rest], owned.at[rest], all_s.at[stage]).wait()
 
 
 def solution(mesh):

time: 83 us -> 82.7 us (level)
  no operation moved by 1% of the time
where the time goes in v8:
time: 82.7 us; the launch traced here: 82.6 us
  Pallas kernels  80.6 us (97%)
  local copies, waits for them, and re-layouts  1.41 us (2%)
    pallas_call x1, Pallas kernels, on_device(): pl.pallas_call(functools.partial(kernel, dims), out_shape=(jax.ShapeDtype...  80.6 us

profile of v8, /device:TPU:1, one launch (start us, length us, event | category | flops | bytes accessed | tf_op | source)
XLA Modules:
  0.0 82.6 jit_solution(14599315214320214321)
XLA Ops:
  0.6 80.6 %shard_map.50 = (f32[1024,128]{1,0:T(8,128)S(1)}, f32[64,128]{1,0:T(8,128)S(1)}) custom-call(f32[1,1024,1024]{2,1,0:T(8,128)} %snap_ref.1, f32[1024,128]{1,0:T(8,128)} %row_ref.1, f32[64,128]{1,0:T(8,128)} %bitcast.3), custom_call_target="tpu_custom_call" | custom-call | tf_op jit(solution)/shard_map/pallas_call | solution.py:346
  81.2 0.8 copy.7
  82.0 0.6 copy.8
